TPU v7x, 512 devices: a whole 4x8x8 slice. The times are simulated.
512 devices in a mesh: replica: 16 (over y_lo, z), fsdp: 32 (over y_hi, x, core).
Axes of the slice: x: 4, y: 8 (y_hi: 4, y_lo: 2; y = y_hi * 2 + y_lo), z: 8, core: 2. Of those that a mesh axis runs over, the one named last changes fastest.
Arguments:
- node_feats: bfloat16 [65536, 1024], P(('replica', 'fsdp')), may hold values from -6 to 6
- neighbor_src: int32 [12, 65536], P(None, ('replica', 'fsdp')), may hold values from 0 to 4095, as said below
- distances: float32 [12, 65536], P(None, ('replica', 'fsdp')), may hold values from 0.8 to 5
- graph_ids: int32 [16, 4096], P('replica', 'fsdp'), may hold values from 0 to 7, never falling along the last dimension, each value on 1 to 1024 neighbouring positions
- msg_weight: bfloat16 [1024, 1024], P('fsdp'), may hold values from -0.1875 to 0.1875
- out_weight: bfloat16 [1024, 1024], P('fsdp'), may hold values from -0.1875 to 0.1875
- radial_weight: float32 [8, 1024], replicated, may hold values from -6 to 6
- cotangent: bfloat16 [65536, 1024], P(('replica', 'fsdp')), may hold values from -6 to 6
- fragment: int32 [1], replicated, may hold values from 0 to 7
Outputs:
- node_out: bfloat16 [65536, 1024], P(('replica', 'fsdp'))
- grad_msg: bfloat16 [16, 1024, 1024], P('replica', 'fsdp')
- grad_out: bfloat16 [16, 1024, 1024], P('replica', 'fsdp')
- outer_sum: float32 [2, 1024, 128], P(None, 'fsdp')
Inputs may be any that keep to these rules, and one draw needn't show every extreme that they name: `neighbor_src`: each neighbour index lies within 32 positions of its own atom's index in the group, never equal to it, and inside the group. `graph_ids`: within each group the graph numbers never fall and every graph has at least one atom.
All inputs are finite; a program needn't handle non-finite values. Where the computation divides by a largest or mean magnitude, that divisor is 1e-20 or more.
Results may differ from a plain program's by a relative error of at most 0.02.
Values may be sent and summed in bfloat16 or wider, within the bound.
A program may use at most 64 MiB of HBM per device.

v0:
```python
import math
import jax
import jax.numpy as jnp
from jax import lax
from jax.sharding import PartitionSpec as P

FRAG = 128
GRAPHS = 8
cutoff = 5.0
sharpness = 2.0
tiny = 1e-06


def with_halo(cells, sides, width):
    for axis, dim in sides:
        count = lax.axis_size(axis)
        ends = count - 1
        head = lax.slice_in_dim(cells, 0, width, axis=dim)
        tail = lax.slice_in_dim(cells, cells.shape[dim] - width, cells.shape[dim], axis=dim)
        cells = jnp.concatenate(
            [
                lax.ppermute(tail, axis, [(i, (i + 1) % count) for i in range(ends)]),
                cells,
                lax.ppermute(head, axis, [((i + 1) % count, i) for i in range(ends)]),
            ],
            axis=dim,
        )
    return cells


def passed_along(value, axis, steps):
    count = lax.axis_size(axis)
    leading, last = (max(0, -steps), min(count, count - steps))
    return lax.ppermute(value, axis, [(source, source + steps) for source in range(leading, last)])


def radial(dist_row, radial_weight):
    basis_count = radial_weight.shape[0]
    centers = cutoff * jnp.arange(basis_count).astype(jnp.float32) / (basis_count - 1)
    envelope = 0.5 * (jnp.cos(jnp.pi * dist_row / cutoff) + 1.0)
    basis = jnp.exp(-sharpness * (dist_row[:, None] - centers[None, :]) ** 2) * envelope[:, None]
    return jnp.dot(
        basis, radial_weight, precision=lax.Precision.HIGHEST, preferred_element_type=jnp.float32
    )


def contract_rows(left, right):
    return lax.dot_general(
        left, right, (((0,), (0,)), ((), ())), preferred_element_type=jnp.float32
    )


def shards(
    node_feats,
    neighbor_src,
    distances,
    graph_ids,
    msg_weight,
    out_weight,
    radial_weight,
    cotangent,
    fragment,
):
    atoms = node_feats.shape[0]
    width = node_feats.shape[1]
    neighbors = neighbor_src.shape[0]
    margin = atoms // 4
    norm = 1.0 / math.sqrt(neighbors)
    first_atom = lax.axis_index("fsdp") * atoms
    empty = jnp.zeros((atoms, width), jnp.float32)
    inputs = node_feats
    projected = jnp.dot(
        inputs,
        lax.all_gather(msg_weight, "fsdp", axis=0, tiled=True),
        preferred_element_type=jnp.float32,
    ).astype(jnp.bfloat16)
    extended = with_halo(projected, (("fsdp", 0),), margin)
    local_src = neighbor_src - first_atom + margin

    def gather_step(k, acc):
        rows = jnp.take(extended, local_src[k], axis=0).astype(jnp.float32)
        return acc + radial(distances[k], radial_weight) * rows

    agg = lax.fori_loop(0, neighbors, gather_step, empty) * norm
    act = jax.nn.silu(agg).astype(jnp.bfloat16)
    inputs = act
    branch_sum = jnp.dot(
        inputs,
        lax.all_gather(out_weight, "fsdp", axis=0, tiled=True),
        preferred_element_type=jnp.float32,
    )
    node_out = (node_feats.astype(jnp.float32) + branch_sum).astype(jnp.bfloat16)
    ids = graph_ids[0]
    onehot = (ids[:, None] == jnp.arange(GRAPHS, dtype=jnp.int32)[None, :]).astype(jnp.float32)
    own_counts = jnp.sum(onehot, axis=0).astype(jnp.int32)
    counts = lax.psum(own_counts, "fsdp")
    weight = jnp.sum(onehot * lax.rsqrt(counts.astype(jnp.float32))[None, :], axis=1)
    dout = (weight[:, None] * cotangent.astype(jnp.float32)).astype(jnp.bfloat16)
    out_rows = lax.psum_scatter(
        contract_rows(act, dout).astype(jnp.bfloat16), "fsdp", scatter_dimension=0, tiled=True
    ).astype(jnp.float32)
    dact = lax.dot_general(
        dout,
        lax.all_gather(out_weight, "fsdp", axis=0, tiled=True),
        (((1,), (1,)), ((), ())),
        preferred_element_type=jnp.float32,
    )
    sig = jax.nn.sigmoid(agg)
    dagg = dact * sig * (1.0 + agg * (1.0 - sig))

    def spread_step(k, acc):
        return acc.at[local_src[k]].add(radial(distances[k], radial_weight) * dagg * norm)

    spread = lax.fori_loop(
        0, neighbors, spread_step, jnp.zeros((atoms + 2 * margin, width), jnp.float32)
    )
    lower_rim = spread[:margin]
    upper_rim = spread[margin + atoms :]
    from_below = passed_along(upper_rim.astype(jnp.bfloat16), "fsdp", 1).astype(upper_rim.dtype)
    from_above = passed_along(lower_rim.astype(jnp.bfloat16), "fsdp", -1).astype(lower_rim.dtype)
    dproj = spread[margin : margin + atoms]
    dproj = dproj.at[:margin].add(from_below)
    dproj = dproj.at[atoms - margin :].add(from_above)
    dproj = dproj.astype(jnp.bfloat16)
    msg_rows = lax.psum_scatter(
        contract_rows(node_feats, dproj).astype(jnp.bfloat16),
        "fsdp",
        scatter_dimension=0,
        tiled=True,
    ).astype(jnp.float32)
    column = fragment[0] * FRAG
    pieces = jnp.stack(
        [
            lax.dynamic_slice_in_dim(msg_rows, column, FRAG, 1),
            lax.dynamic_slice_in_dim(out_rows, column, FRAG, 1),
        ]
    )
    scale = (jnp.max(jnp.abs(pieces), axis=-1, keepdims=True) + tiny).astype(jnp.bfloat16)
    code = (pieces / scale.astype(jnp.float32)).astype(jnp.bfloat16)
    outer_sum = lax.psum(
        (scale.astype(jnp.float32) * code.astype(jnp.float32)).astype(jnp.bfloat16), "replica"
    ).astype(jnp.float32)
    return (
        node_out,
        msg_rows.astype(jnp.bfloat16)[None],
        out_rows.astype(jnp.bfloat16)[None],
        outer_sum,
    )


def solution(mesh):
    placed = (
        P(("replica", "fsdp"), None),
        P(None, ("replica", "fsdp")),
        P(None, ("replica", "fsdp")),
        P("replica", "fsdp"),
        P("fsdp", None),
        P("fsdp", None),
        P(),
        P(("replica", "fsdp"), None),
        P(),
    )
    return jax.shard_map(
        shards,
        mesh=mesh,
        in_specs=placed,
        out_specs=(
            P(("replica", "fsdp"), None),
            P("replica", "fsdp", None),
            P("replica", "fsdp", None),
            P(None, "fsdp", None),
        ),
        check_vma=False,
    )
```

profile of v0, /device:TPU:8, one launch (start us, length us, event | category | flops | bytes accessed | tf_op | source)
XLA Modules:
  0.0 413.5 jit_solution(17825532584873003960)
XLA Ops:
  9.5 18.2 %psum.14 = s32[8]{0:T(128)S(1)} all-reduce(s32[8]{0:T(128)S(1)} %convert_element_type.127), channel_id=1, replica_groups=mesh['replica'=16,'fsdp'=32] {'fsdp'}, use_global_device_ids=true, to_apply=%region_3.4 | all-reduce | flops 8 | bytes 64 | tf_op jit(solution)/shard_map/psum | solution.py:96
  28.4 45.7 %all-gather.3.cloned.1.call-done = bf16[1024,1024]{1,0:T(8,128)(2,1)} async-done(((bf16[32,1024]{1,0:T(8,128)(2,1)}), bf16[1024,1024]{1,0:T(8,128)(2,1)}) %all-gather.3.cloned.1.call-update) | async-done | bytes 2097168 | tf_op jit(solution)/shard_map/all_gather | solution.py:74
  74.1 2.1 convolution_convert_fusion.1
  76.2 2.1 collective-permute-start
  78.4 1.3 collective-permute-start.1
  79.8 2.2 collective-permute-done.1
  82.0 29.7 %while.34 = (s32[]{:T(128)}, f32[128,1024]{1,0:T(8,128)S(1)}, f32[12,128]{1,0:T(8,128)}, f32[8,1024]{1,0:T(8,128)S(1)}, s32[12,128]{1,0:T(8,128)S(1)}, /*index=5*/bf16[192,1024]{1,0:T(8,128)(2,1)S(1)}, s32[]{:T(128)}, s32[]{:T(128)}) while((s32[]{:T(128)}, f32[128,1024]{1,0:T(8,128)S(1)}, f32[12,128]{1,0:T(8,128)}, ...), condition=%wide.region_1.0_spmd.clone, body=%wide.region_0.1_spmd.clone.sunk | while | flops 13244947 | bytes 1877427 | solution.py:84
  111.7 2.1 convolution_convert_fusion
  113.9 20.3 %all-gather.5.cloned.1.call-done = bf16[1024,1024]{1,0:T(8,128)(2,1)} async-done(((bf16[32,1024]{1,0:T(8,128)(2,1)}), bf16[1024,1024]{1,0:T(8,128)(2,1)}) %all-gather.5.cloned.1.call-update) | async-done | bytes 2097168 | tf_op jit(solution)/shard_map/all_gather | solution.py:89
  134.2 2.5 fusion.24
  136.7 41.1 %while.33 = (s32[]{:T(128)}, f32[192,1024]{1,0:T(8,128)S(1)}, s32[12,128]{1,0:T(8,128)S(1)}, f32[12,128]{1,0:T(8,128)}, f32[8,1024]{1,0:T(8,128)S(1)}, /*index=5*/f32[128,1024]{1,0:T(8,128)S(1)}, s32[]{:T(128)}) while((s32[]{:T(128)}, f32[192,1024]{1,0:T(8,128)S(1)}, s32[12,128]{1,0:T(8,128)S(1)}, f32[12,128]{1,0:T(8,128)}, ...), condition=%wide.region_7.8_spmd, body=%wide.region_5.7_spmd.sunk | while | flops 12981010 | bytes 2658461 | solution.py:114
  138.2 1.9 scatter_fusion
  141.6 1.9 scatter_fusion
  145.0 1.9 scatter_fusion
  148.5 1.9 scatter_fusion
  151.9 1.9 scatter_fusion
  155.3 1.9 scatter_fusion
  158.7 1.9 scatter_fusion
  162.2 1.9 scatter_fusion
  165.6 1.9 scatter_fusion
  169.0 1.9 scatter_fusion
  172.4 1.9 scatter_fusion
  175.9 1.9 scatter_fusion
  177.9 2.1 collective-permute-start.2
  180.1 1.3 collective-permute-start.3
  181.4 2.1 collective-permute-done.3
  184.3 2.6 copy.22
  188.5 1.2 fusion.25
  189.7 47.1 %reduce-scatter.5.cloned.1.call-done = bf16[32,1024]{1,0:T(8,128)(2,1)} async-done(((bf16[1024,1024]{1,0:T(8,128)(2,1)}), bf16[32,1024]{1,0:T(8,128)(2,1)}) %reduce-scatter.5.cloned.1.call-update) | async-done | bytes 65552 | tf_op jit(solution)/shard_map/reduce_scatter | solution.py:99
  237.5 101.5 %reduce-scatter.7.cloned.1.call-done = bf16[32,1024]{1,0:T(8,128)(2,1)} async-done(((bf16[1024,1024]{1,0:T(8,128)(2,1)}), bf16[32,1024]{1,0:T(8,128)(2,1)}) %reduce-scatter.7.cloned.1.call-update) | async-done | bytes 65552 | tf_op jit(solution)/shard_map/reduce_scatter | solution.py:125
  339.9 64.7 %psum.15 = bf16[2,32,128]{2,1,0:T(8,128)(2,1)S(1)} all-reduce(bf16[2,32,128]{2,1,0:T(8,128)(2,1)S(1)} %multiply_convert_fusion.4), channel_id=1, replica_groups=mesh['replica'=16,'fsdp'=32] {'replica'}, use_global_device_ids=true, to_apply=%region_11.12 | all-reduce | flops 8192 | bytes 32768 | tf_op jit(solution)/shard_map/psum | solution.py:140
  405.2 1.0 copy.23
  (174 shorter events, 54.5 us)
Async XLA Ops:
  7.2 72.5 %copy-start.4 = (s32[1,128]{1,0:T(1,128)S(1)}, s32[1,128]{1,0:T(1,128)}, u32[]{:S(2)}) copy-start(s32[1,128]{1,0:T(1,128)} %param.20) | copy-start | bytes 1540
  7.2 74.8 %copy-start = (f32[8,1024]{1,0:T(8,128)S(1)}, f32[8,1024]{1,0:T(8,128)}, u32[]{:S(2)}) copy-start(f32[8,1024]{1,0:T(8,128)} %param.23) | copy-start | bytes 98308
  7.2 66.9 %all-gather.3.cloned.1.call-start = ((), (), s32[]{:S(2)}) async-start(), calls=%async_computation.2 | async-start | bytes 2162688 | tf_op jit(solution)/shard_map/all_gather | solution.py:74
  7.9 126.2 %all-gather.5.cloned.1.call-start = ((), (), s32[]{:S(2)}) async-start(), calls=%async_computation.3 | async-start | bytes 2162688 | tf_op jit(solution)/shard_map/all_gather | solution.py:89
  8.7 228.1 %reduce-scatter.5.cloned.1.call-start = ((), (), s32[]{:S(2)}) async-start(), calls=%async_computation.4 | async-start | bytes 2162688 | tf_op jit(solution)/shard_map/reduce_scatter | solution.py:99
  76.2 3.5 collective-permute-start
  78.4 3.6 collective-permute-start.1
  82.0 29.7 %copy-start.3 = (bf16[128,1024]{1,0:T(8,128)(2,1)S(1)}, bf16[128,1024]{1,0:T(8,128)(2,1)}, u32[]{:S(2)}) copy-start(bf16[128,1024]{1,0:T(8,128)(2,1)} %param.24) | copy-start | bytes 786436
  113.8 225.2 %reduce-scatter.7.cloned.1.call-start = ((), (), s32[]{:S(2)}) async-start(), calls=%async_computation.5 | async-start | bytes 2162688 | tf_op jit(solution)/shard_map/reduce_scatter | solution.py:125
  177.8 5.8 %copy-start.1 = (bf16[128,1024]{1,0:T(8,128)(2,1)S(1)}, bf16[128,1024]{1,0:T(8,128)(2,1)}, u32[]{:S(2)}) copy-start(bf16[128,1024]{1,0:T(8,128)(2,1)} %param.17) | copy-start | bytes 786436
  177.9 3.5 collective-permute-start.2
  180.1 3.5 collective-permute-start.3
  186.9 1.6 copy-start.2
Sparse Core Ops, SparseCore 0:
  11.1 62.8 all-gather.2
  77.2 56.9 all-gather.4
  139.1 97.5 reduce-scatter.4
  241.0 97.8 reduce-scatter.6
where the time goes:
time: 415 us; the launch traced here: 413 us
  waiting for transfers between devices  220 us (53%)
  blocking collectives  82.8 us (20%)
  other arithmetic  45.4 us (11%)
  matrix products  26.5 us (6%)
  local copies, waits for them, and re-layouts  15.6 us (4%)
  between operations  14.8 us (4%)
  starting transfers between devices  6.99 us (2%)
    reduce_scatter x1, waiting for transfers between devices, shards(): lax.psum_scatter(contract_rows(node_feats, dproj).astype(jnp.bfloat16), '...  102 us
    psum x1, blocking collectives, shards(): lax.psum((scale.astype(jnp.float32) * code.astype(jnp.float32)).astype(jn...  64.7 us
    reduce_scatter x1, waiting for transfers between devices, shards(): lax.psum_scatter(contract_rows(act, dout).astype(jnp.bfloat16), 'fsdp', s...  47.1 us
    all_gather x1, waiting for transfers between devices, shards(): lax.all_gather(msg_weight, 'fsdp', axis=0, tiled=True)  45.7 us
    scatter-add x12, other arithmetic, spread_step(): acc.at[local_src[k]].add(radial(distances[k], radial_weight) * dagg * norm)  23.1 us
    all_gather x1, waiting for transfers between devices, shards(): lax.all_gather(out_weight, 'fsdp', axis=0, tiled=True)  20.3 us
    psum x1, blocking collectives, shards(): counts = lax.psum(own_counts, 'fsdp')  18.2 us
    dot_general x24, matrix products, radial(): jnp.dot(basis, radial_weight, precision=lax.Precision.HIGHEST, preferred_...  17.9 us
  transfers between devices with their start and end apart: 8, of which 6 were waited for; matrix products, arithmetic and copies ran while one was open for 20% of the time, Pallas kernels for 0%

commit v1 on v0

--- a/solution.py
+++ b/solution.py
@@ -137,8 +137,11 @@
     )
     scale = (jnp.max(jnp.abs(pieces), axis=-1, keepdims=True) + tiny).astype(jnp.bfloat16)
     code = (pieces / scale.astype(jnp.float32)).astype(jnp.bfloat16)
-    outer_sum = lax.psum(
-        (scale.astype(jnp.float32) * code.astype(jnp.float32)).astype(jnp.bfloat16), "replica"
+    outer_sum = jnp.sum(
+        lax.all_gather(
+            (scale.astype(jnp.float32) * code.astype(jnp.float32)).astype(jnp.bfloat16), "replica"
+        ),
+        axis=0,
     ).astype(jnp.float32)
     return (
         node_out,

time: 415 us -> 386 us (0.930)
  blocking collectives: 82.8 us -> 54.1 us
    psum x1 -> x0, blocking collectives: 64.7 us -> none  [shards(): lax.psum((scale.astype(jnp.float32) * code.astype(jnp.float32)).astype(jn...]
    all_gather x0 -> x1, blocking collectives: none -> 35.9 us  [shards(): lax.all_gather((scale.astype(jnp.float32) * code.astype(jnp.float32)).ast...]
  transfers between devices with their start and end apart: 8 -> 8, of which waited for: 6 -> 6; matrix products, arithmetic and copies ran while one was open for 20% -> 22% of each run, Pallas kernels for 0% -> 0%
where the time goes in v1:
time: 386 us; the launch traced here: 385 us
  waiting for transfers between devices  220 us (57%)
  blocking collectives  54.1 us (14%)
  other arithmetic  45.4 us (12%)
  matrix products  26.5 us (7%)
  local copies, waits for them, and re-layouts  15.6 us (4%)
  between operations  14.8 us (4%)
  starting transfers between devices  6.99 us (2%)
    reduce_scatter x1, waiting for transfers between devices, shards(): lax.psum_scatter(contract_rows(node_feats, dproj).astype(jnp.bfloat16), '...  102 us
    reduce_scatter x1, waiting for transfers between devices, shards(): lax.psum_scatter(contract_rows(act, dout).astype(jnp.bfloat16), 'fsdp', s...  47.1 us
    all_gather x1, waiting for transfers between devices, shards(): lax.all_gather(msg_weight, 'fsdp', axis=0, tiled=True)  45.7 us
    all_gather x1, blocking collectives, shards(): lax.all_gather((scale.astype(jnp.float32) * code.astype(jnp.float32)).ast...  35.9 us
    scatter-add x12, other arithmetic, spread_step(): acc.at[local_src[k]].add(radial(distances[k], radial_weight) * dagg * norm)  23.1 us
    all_gather x1, waiting for transfers between devices, shards(): lax.all_gather(out_weight, 'fsdp', axis=0, tiled=True)  20.3 us
    psum x1, blocking collectives, shards(): counts = lax.psum(own_counts, 'fsdp')  18.2 us
    dot_general x24, matrix products, radial(): jnp.dot(basis, radial_weight, precision=lax.Precision.HIGHEST, preferred_...  17.9 us
  transfers between devices with their start and end apart: 8, of which 6 were waited for; matrix products, arithmetic and copies ran while one was open for 22% of the time, Pallas kernels for 0%

profile of v1, /device:TPU:8, one launch (start us, length us, event | category | flops | bytes accessed | tf_op | source)
XLA Modules:
  0.0 384.7 jit_solution(12935379179908449124)
XLA Ops:
  9.5 18.2 %psum.7 = s32[8]{0:T(128)S(1)} all-reduce(s32[8]{0:T(128)S(1)} %convert_element_type.150), channel_id=1, replica_groups=mesh['replica'=16,'fsdp'=32] {'fsdp'}, use_global_device_ids=true, to_apply=%region_3.4 | all-reduce | flops 8 | bytes 64 | tf_op jit(solution)/shard_map/psum | solution.py:96
  28.4 45.7 %all-gather.3.cloned.1.call-done = bf16[1024,1024]{1,0:T(8,128)(2,1)} async-done(((bf16[32,1024]{1,0:T(8,128)(2,1)}), bf16[1024,1024]{1,0:T(8,128)(2,1)}) %all-gather.3.cloned.1.call-update) | async-done | bytes 2097168 | tf_op jit(solution)/shard_map/all_gather | solution.py:74
  74.1 2.1 convolution_convert_fusion.1
  76.2 2.1 collective-permute-start
  78.4 1.3 collective-permute-start.1
  79.8 2.2 collective-permute-done.1
  82.0 29.7 %while.34 = (s32[]{:T(128)}, f32[128,1024]{1,0:T(8,128)S(1)}, f32[12,128]{1,0:T(8,128)}, f32[8,1024]{1,0:T(8,128)S(1)}, s32[12,128]{1,0:T(8,128)S(1)}, /*index=5*/bf16[192,1024]{1,0:T(8,128)(2,1)S(1)}, s32[]{:T(128)}, s32[]{:T(128)}) while((s32[]{:T(128)}, f32[128,1024]{1,0:T(8,128)S(1)}, f32[12,128]{1,0:T(8,128)}, ...), condition=%wide.region_1.0_spmd.clone, body=%wide.region_0.1_spmd.clone.sunk | while | flops 13244947 | bytes 1877427 | solution.py:84
  111.7 2.1 convolution_convert_fusion
  113.9 20.3 %all-gather.5.cloned.1.call-done = bf16[1024,1024]{1,0:T(8,128)(2,1)} async-done(((bf16[32,1024]{1,0:T(8,128)(2,1)}), bf16[1024,1024]{1,0:T(8,128)(2,1)}) %all-gather.5.cloned.1.call-update) | async-done | bytes 2097168 | tf_op jit(solution)/shard_map/all_gather | solution.py:89
  134.2 2.5 fusion.24
  136.7 41.1 %while.33 = (s32[]{:T(128)}, f32[192,1024]{1,0:T(8,128)S(1)}, s32[12,128]{1,0:T(8,128)S(1)}, f32[12,128]{1,0:T(8,128)}, f32[8,1024]{1,0:T(8,128)S(1)}, /*index=5*/f32[128,1024]{1,0:T(8,128)S(1)}, s32[]{:T(128)}) while((s32[]{:T(128)}, f32[192,1024]{1,0:T(8,128)S(1)}, s32[12,128]{1,0:T(8,128)S(1)}, f32[12,128]{1,0:T(8,128)}, ...), condition=%wide.region_7.8_spmd, body=%wide.region_5.7_spmd.sunk | while | flops 12981010 | bytes 2658461 | solution.py:114
  138.2 1.9 scatter_fusion
  141.6 1.9 scatter_fusion
  145.0 1.9 scatter_fusion
  148.5 1.9 scatter_fusion
  151.9 1.9 scatter_fusion
  155.3 1.9 scatter_fusion
  158.7 1.9 scatter_fusion
  162.2 1.9 scatter_fusion
  165.6 1.9 scatter_fusion
  169.0 1.9 scatter_fusion
  172.4 1.9 scatter_fusion
  175.9 1.9 scatter_fusion
  177.9 2.1 collective-permute-start.2
  180.1 1.3 collective-permute-start.3
  181.4 2.1 collective-permute-done.3
  184.3 2.6 copy.24
  188.5 1.2 fusion.25
  189.7 47.1 %reduce-scatter.5.cloned.1.call-done = bf16[32,1024]{1,0:T(8,128)(2,1)} async-done(((bf16[1024,1024]{1,0:T(8,128)(2,1)}), bf16[32,1024]{1,0:T(8,128)(2,1)}) %reduce-scatter.5.cloned.1.call-update) | async-done | bytes 65552 | tf_op jit(solution)/shard_map/reduce_scatter | solution.py:99
  237.5 101.5 %reduce-scatter.7.cloned.1.call-done = bf16[32,1024]{1,0:T(8,128)(2,1)} async-done(((bf16[1024,1024]{1,0:T(8,128)(2,1)}), bf16[32,1024]{1,0:T(8,128)(2,1)}) %reduce-scatter.7.cloned.1.call-update) | async-done | bytes 65552 | tf_op jit(solution)/shard_map/reduce_scatter | solution.py:125
  339.8 1.0 copy.25
  341.6 35.9 %all_gather.13 = bf16[16,2,32,128]{3,2,1,0:T(8,128)(2,1)S(1)} all-gather(bf16[1,2,32,128]{3,2,1,0:T(8,128)(2,1)S(1)} %multiply_convert_fusion.4), channel_id=1, replica_groups=mesh['replica'=16,'fsdp'=32] {'replica'}, dimensions={0}, use_global_device_ids=true | all-gather | bytes 278528 | tf_op jit(solution)/shard_map/all_gather | solution.py:141
  (175 shorter events, 54.5 us)
Async XLA Ops:
  7.2 72.5 %copy-start.4 = (s32[1,128]{1,0:T(1,128)S(1)}, s32[1,128]{1,0:T(1,128)}, u32[]{:S(2)}) copy-start(s32[1,128]{1,0:T(1,128)} %param.20) | copy-start | bytes 1540
  7.2 74.8 %copy-start = (f32[8,1024]{1,0:T(8,128)S(1)}, f32[8,1024]{1,0:T(8,128)}, u32[]{:S(2)}) copy-start(f32[8,1024]{1,0:T(8,128)} %param.23) | copy-start | bytes 98308
  7.2 66.9 %all-gather.3.cloned.1.call-start = ((), (), s32[]{:S(2)}) async-start(), calls=%async_computation.2 | async-start | bytes 2162688 | tf_op jit(solution)/shard_map/all_gather | solution.py:74
  7.9 126.2 %all-gather.5.cloned.1.call-start = ((), (), s32[]{:S(2)}) async-start(), calls=%async_computation.3 | async-start | bytes 2162688 | tf_op jit(solution)/shard_map/all_gather | solution.py:89
  8.7 228.1 %reduce-scatter.5.cloned.1.call-start = ((), (), s32[]{:S(2)}) async-start(), calls=%async_computation.4 | async-start | bytes 2162688 | tf_op jit(solution)/shard_map/reduce_scatter | solution.py:99
  76.2 3.5 collective-permute-start
  78.4 3.6 collective-permute-start.1
  82.0 29.7 %copy-start.3 = (bf16[128,1024]{1,0:T(8,128)(2,1)S(1)}, bf16[128,1024]{1,0:T(8,128)(2,1)}, u32[]{:S(2)}) copy-start(bf16[128,1024]{1,0:T(8,128)(2,1)} %param.24) | copy-start | bytes 786436
  113.8 225.1 %reduce-scatter.7.cloned.1.call-start = ((), (), s32[]{:S(2)}) async-start(), calls=%async_computation.5 | async-start | bytes 2162688 | tf_op jit(solution)/shard_map/reduce_scatter | solution.py:125
  177.8 5.8 %copy-start.1 = (bf16[128,1024]{1,0:T(8,128)(2,1)S(1)}, bf16[128,1024]{1,0:T(8,128)(2,1)}, u32[]{:S(2)}) copy-start(bf16[128,1024]{1,0:T(8,128)(2,1)} %param.17) | copy-start | bytes 786436
  177.9 3.5 collective-permute-start.2
  180.1 3.5 collective-permute-start.3
  186.9 1.6 copy-start.2
Sparse Core Ops, SparseCore 0:
  11.1 62.8 all-gather.2
  77.2 56.9 all-gather.4
  139.1 97.5 reduce-scatter.4
  241.0 97.8 reduce-scatter.6
